TPU v7x, 256 devices: a whole 4x4x8 slice. The times are simulated.
256 devices in a mesh: row: 8 (over x, y_hi), col: 32 (over z, y_lo, core).
Axes of the slice: x: 4, y: 4 (y_hi: 2, y_lo: 2; y = y_hi * 2 + y_lo), z: 8, core: 2. Of those that a mesh axis runs over, the one named last changes fastest.
Arguments:
- left_panel: float32 [4096, 8192], P('col', 'row'), may hold values from -6 to 6
- right_panel: float32 [4096, 16384], P('row', 'col'), may hold values from -0.09375 to 0.09375
- arc_basis: float32 [4096, 256], replicated, as said below
- normal_block: float32 [8192, 16384], P('row', 'col'), may hold values from -6 to 6
Outputs:
- updated_block: float32 [8192, 16384], P('row', 'col')
- left_reduced: float32 [4096, 8192], P('col', 'row')
- right_reduced: float32 [4096, 16384], P('row', 'col')
Inputs may be any that keep to these rules, and one draw needn't show every extreme that they name: arc_basis has orthonormal columns: arc_basis^T arc_basis equals the 256 x 256 identity within float32 rounding.
All inputs are finite; a program needn't handle non-finite values.
Results may differ from a plain program's by a relative error of at most 0.00005.
Values sent between devices are 32-bit elements; how exact they have to be, the bound alone decides.
No kernel may reach another device: no remote copies, remote signals or barrier semaphores. Data moves between devices by JAX's collectives and lax.ppermute only.
A program may use at most 128 MiB of HBM per device.

v0:
```python
import jax
import jax.numpy as jnp
from jax import lax
from jax.sharding import Mesh
from jax.sharding import PartitionSpec as P

COL = ("col_0", "col_1", "col_2")


def split_up(shard, dim, devices):
    dims = shard.shape
    tiles = shard.reshape(*dims[:dim], devices, dims[dim] // devices, *dims[dim + 1 :])
    return jnp.moveaxis(tiles, dim, 0)


def summed_on_arrival(shard, axis, dim):
    devices = lax.axis_size(axis)
    tiles = lax.all_to_all(split_up(shard, dim, devices), axis, 0, 0, tiled=True)
    return jnp.sum(tiles, axis=0)


def sum_in_two_steps(shard, axes, dim):
    far, near = axes
    own = summed_on_arrival(split_up(shard, dim, lax.axis_size(far)), near, dim + 1)
    return jnp.sum(lax.all_to_all(own, far, 0, 0, tiled=True), axis=0)


def rows_for(lines, devices):
    spare = -len(lines) % devices
    return jnp.pad(lines, [(0, spare)] + [(0, 0)] * (lines.ndim - 1))


def copy_for_each(shard, axis):
    copies = jnp.broadcast_to(shard, (lax.axis_size(axis), *shard.shape))
    return lax.all_to_all(copies, axis, split_axis=0, concat_axis=0, tiled=True)


def joined_along(tiles, dim):
    dims = list(tiles.shape[1:])
    dims[dim] *= tiles.shape[0]
    return jnp.moveaxis(tiles, 0, dim).reshape(dims)


def gathered_by_axis(shard, axes, dim):
    far, near = axes
    leading = copy_for_each(shard, far)
    tiles = jnp.swapaxes(copy_for_each(leading, near), 0, 1)
    return joined_along(tiles.reshape(-1, *shard.shape), dim)


def nested_sum(shard, axes):
    lines = shard.reshape(-1, shard.shape[-1])
    own = sum_in_two_steps(
        rows_for(lines, lax.axis_size(axes[0]) * lax.axis_size(axes[1])), axes, 0
    )
    whole = gathered_by_axis(own, axes, 0)
    return whole[: len(lines)].reshape(shard.shape)


def taken_together(shard, axis):
    return copy_for_each(shard, axis).sum(axis=0)


def inner_product(first, second):
    return lax.dot_general(
        first,
        second,
        (((0,), (0,)), ((), ())),
        precision=lax.Precision.HIGHEST,
        preferred_element_type=jnp.float32,
    )


def plain_product(first, second):
    return jnp.dot(
        first, second, precision=lax.Precision.HIGHEST, preferred_element_type=jnp.float32
    )


def local(left_panel, right_panel, arc_basis, normal_block):
    left_count = left_panel.shape[0]
    right_count = right_panel.shape[0]
    col_index = lax.axis_index(COL)
    row_index = lax.axis_index("row")
    basis_left = lax.dynamic_slice_in_dim(arc_basis, col_index * left_count, left_count, 0)
    basis_right = lax.dynamic_slice_in_dim(arc_basis, row_index * right_count, right_count, 0)
    left_coef = nested_sum(inner_product(basis_left, left_panel), (("col_0", "col_1"), "col_2"))
    right_coef = taken_together(inner_product(basis_right, right_panel), "row")
    left_reduced = left_panel - plain_product(basis_left, left_coef)
    right_reduced = right_panel - plain_product(basis_right, right_coef)
    initial = normal_block - inner_product(left_coef, right_coef)
    left_whole = lax.all_gather(left_panel, COL, axis=0, tiled=True)
    updated_block = initial + inner_product(
        left_whole, lax.all_gather(right_panel, "row", axis=0, tiled=True)
    )
    return (updated_block, left_reduced, right_reduced)


def solution(mesh):
    split = Mesh(
        mesh.devices.reshape(mesh.shape["row"], 8, 2, 2), ("row", "col_0", "col_1", "col_2")
    )
    in_specs = (P(COL, "row"), P("row", COL), P(), P("row", COL))
    out_specs = (P("row", COL), P(COL, "row"), P("row", COL))
    return jax.shard_map(local, mesh=split, in_specs=in_specs, out_specs=out_specs, check_vma=False)
```

profile of v0, /device:TPU:1, one launch (start us, length us, event | category | flops | bytes accessed | tf_op | source)
XLA Modules:
  0.0 318.7 jit_solution(193873724330745306)
XLA Ops:
  7.2 0.0 all-gather.5.cloned.1.call-start
  7.2 0.7 all-gather.5.cloned.1.call-update
  7.9 0.0 all-gather.3.cloned.1.call-start
  7.9 0.7 all-gather.3.cloned.1.call-update
  8.7 2.1 fusion.4
  10.8 0.0 copy-start
  10.8 0.1 copy.12
  10.9 7.6 %all_to_all.25 = f32[2,16,8,1024]{3,2,1,0:T(8,128)S(1)} all-to-all(f32[2,16,8,1024]{3,2,1,0:T(8,128)S(1)} %bitcast.18), channel_id=1, replica_groups=mesh['row'=8,'col_0'=8,'col_1'=2,'col_2'=2] {'col_2'}, dimensions={0} | all-to-all | bytes 2097152 | tf_op jit(solution)/shard_map/all_to_all | solution.py:18
  18.5 0.1 reduce_sum.27
  18.6 23.4 %all_to_all.26 = f32[16,8,1024]{2,1,0:T(8,128)S(1)} all-to-all(f32[16,8,1024]{2,1,0:T(8,128)S(1)} %reduce_sum.27), channel_id=1, replica_groups=mesh['row'=8,'col_0'=8,'col_1'=2,'col_2'=2] {'col_0','col_1'}, dimensions={0} | all-to-all | bytes 1048576 | tf_op jit(solution)/shard_map/all_to_all | solution.py:25
  42.0 0.8 broadcast_in_dim.9
  42.9 4.5 %all-to-all-start.2 = ((f32[16,8,1024]{2,1,0:T(8,128)}), f32[16,8,1024]{2,1,0:T(8,128)S(1)}, u32[]{:S(2)}, u32[]{:S(2)}) async-start(f32[16,8,1024]{2,1,0:T(8,128)} %broadcast_in_dim.9), calls=%async_computation.2 | async-start | bytes 1048576 | tf_op jit(solution)/shard_map/all_to_all | solution.py:35
  47.4 0.0 copy-done
  47.4 2.1 fusion.1
  49.5 13.1 %all-to-all-done.2 = f32[16,8,1024]{2,1,0:T(8,128)S(1)} async-done(((f32[16,8,1024]{2,1,0:T(8,128)}), f32[16,8,1024]{2,1,0:T(8,128)S(1)}, u32[]{:S(2)}, u32[]{:S(2)}) %all-to-all-start.2) | async-done | bytes 524320 | tf_op jit(solution)/shard_map/all_to_all | solution.py:35
  62.6 0.1 broadcast_in_dim.10
  62.8 8.0 %all_to_all.27 = f32[2,16,8,1024]{3,2,1,0:T(8,128)} all-to-all(f32[2,16,8,1024]{3,2,1,0:T(8,128)S(1)} %broadcast_in_dim.10), channel_id=1, replica_groups=mesh['row'=8,'col_0'=8,'col_1'=2,'col_2'=2] {'col_2'}, dimensions={0} | all-to-all | bytes 2097152 | tf_op jit(solution)/shard_map/all_to_all | solution.py:35
  70.7 2.5 broadcast_in_dim.11
  73.2 0.0 copy-start.1
  73.2 6.5 %all-to-all-start.4 = ((f32[8,256,512]{2,1,0:T(8,128)}), f32[8,256,512]{2,1,0:T(8,128)}, u32[]{:S(2)}, u32[]{:S(2)}) async-start(f32[8,256,512]{2,1,0:T(8,128)} %broadcast_in_dim.11), calls=%async_computation.4 | async-start | bytes 8388608 | tf_op jit(solution)/shard_map/all_to_all | solution.py:35
  79.7 1.3 copy.10
  81.0 0.0 copy-done.1
  81.0 2.4 convolution_subtract_fusion.1
  83.4 56.6 %all-to-all-done.4 = f32[8,256,512]{2,1,0:T(8,128)} async-done(((f32[8,256,512]{2,1,0:T(8,128)}), f32[8,256,512]{2,1,0:T(8,128)}, u32[]{:S(2)}, u32[]{:S(2)}) %all-to-all-start.4) | async-done | bytes 4194336 | tf_op jit(solution)/shard_map/all_to_all | solution.py:35
  140.0 2.7 reduce_sum.29
  142.7 3.0 convolution_subtract_fusion
  145.7 32.2 %all-gather.5.cloned.1.call-done = f32[4096,512]{1,0:T(8,128)} async-done(((f32[512,512]{1,0:T(8,128)}), f32[4096,512]{1,0:T(8,128)}) %all-gather.5.cloned.1.call-update) | async-done | bytes 8388624 | tf_op jit(solution)/shard_map/all_gather | solution.py:94
  178.0 100.4 %all-gather.3.cloned.1.call-done = f32[4096,1024]{1,0:T(8,128)} async-done(((f32[128,1024]{1,0:T(8,128)}), f32[4096,1024]{1,0:T(8,128)}) %all-gather.3.cloned.1.call-update) | async-done | bytes 16777232 | tf_op jit(solution)/shard_map/all_gather | solution.py:92
  278.4 0.0 copy-start.2
  278.4 30.0 %fusion.10 = f32[1024,512]{1,0:T(8,128)S(1)} fusion(f32[4096,1024]{1,0:T(8,128)} %all-gather.3.cloned.1.call-done, f32[4096,512]{1,0:T(8,128)} %all-gather.5.cloned.1.call-done), kind=kOutput, calls=%fused_computation.14 | convolution fusion | flops 25769803776 | bytes 27262976 | tf_op jit(solution)/shard_map/dot_general | solution.py:65
  308.4 0.0 copy-done.2
  308.4 3.4 %subtract_add_fusion = f32[1024,512]{1,0:T(8,128)} fusion(f32[1024,512]{1,0:T(8,128)S(1)} %fusion.10, f32[1024,512]{1,0:T(8,128)S(1)} %copy-done.2, f32[256,1024]{1,0:T(8,128)S(1)} %bitcast.16, f32[256,512]{1,0:T(8,128)S(1)} %reduce_sum.29), kind=kOutput, calls=%fused_computation | convolution fusion | flops 1611661312 | bytes 7864320 | tf_op jit(solution)/shard_map/dot_general | solution.py:65
  (1 shorter events, 0.0 us)
Async XLA Ops:
  7.2 170.8 %all-gather.5.cloned.1.call-start = ((), (), s32[]{:S(2)}) async-start(), calls=%async_computation.6 | async-start | bytes 9437184 | tf_op jit(solution)/shard_map/all_gather | solution.py:94
  7.9 270.5 %all-gather.3.cloned.1.call-start = ((), (), s32[]{:S(2)}) async-start(), calls=%async_computation.5 | async-start | bytes 17301504 | tf_op jit(solution)/shard_map/all_gather | solution.py:92
  10.8 36.6 %copy-start = (f32[512,512]{1,0:T(8,128)S(1)}, f32[512,512]{1,0:T(8,128)}, u32[]{:S(2)}) copy-start(f32[512,512]{1,0:T(8,128)} %param.5) | copy-start | bytes 3145732
  42.9 19.8 %all-to-all-start.2 = ((f32[16,8,1024]{2,1,0:T(8,128)}), f32[16,8,1024]{2,1,0:T(8,128)S(1)}, u32[]{:S(2)}, u32[]{:S(2)}) async-start(f32[16,8,1024]{2,1,0:T(8,128)} %broadcast_in_dim.9), calls=%async_computation.2 | async-start | bytes 1048576 | tf_op jit(solution)/shard_map/all_to_all | solution.py:35
  73.2 7.8 %copy-start.1 = (f32[128,1024]{1,0:T(8,128)S(1)}, f32[128,1024]{1,0:T(8,128)}, u32[]{:S(2)}) copy-start(f32[128,1024]{1,0:T(8,128)} %param.4) | copy-start | bytes 1572868
  73.2 66.8 %all-to-all-start.4 = ((f32[8,256,512]{2,1,0:T(8,128)}), f32[8,256,512]{2,1,0:T(8,128)}, u32[]{:S(2)}, u32[]{:S(2)}) async-start(f32[8,256,512]{2,1,0:T(8,128)} %broadcast_in_dim.11), calls=%async_computation.4 | async-start | bytes 8388608 | tf_op jit(solution)/shard_map/all_to_all | solution.py:35
  278.4 30.1 %copy-start.2 = (f32[1024,512]{1,0:T(8,128)S(1)}, f32[1024,512]{1,0:T(8,128)}, u32[]{:S(2)}) copy-start(f32[1024,512]{1,0:T(8,128)} %param.7) | copy-start | bytes 6291460
Sparse Core Ops, SparseCore 0:
  10.6 167.2 all-gather.4
  179.8 98.5 all-gather.2
where the time goes:
time: 319 us
  waiting for transfers between devices  204 us (64%)
  matrix products  43.1 us (14%)
  blocking collectives  38.9 us (12%)
  between operations  14.2 us (4%)
  starting transfers between devices  11.1 us (3%)
  local copies, waits for them, and re-layouts  4.85 us (2%)
    all_gather x1, waiting for transfers between devices, local(): left_whole = lax.all_gather(left_panel, COL, axis=0, tiled=True)  100 us
    all_to_all x2, waiting for transfers between devices, copy_for_each(): return lax.all_to_all(copies, axis, split_axis=0, concat_axis=0, tiled=True)  69.7 us
    dot_general x4, matrix products, inner_product(): lax.dot_general(first, second, (((0,), (0,)), ((), ())), precision=lax.Pr...  37.7 us
    all_gather x1, waiting for transfers between devices, local(): lax.all_gather(right_panel, 'row', axis=0, tiled=True)  32.2 us
    all_to_all x1, blocking collectives, sum_in_two_steps(): return jnp.sum(lax.all_to_all(own, far, 0, 0, tiled=True), axis=0)  23.4 us
    all_to_all x2, starting transfers between devices, copy_for_each(): return lax.all_to_all(copies, axis, split_axis=0, concat_axis=0, tiled=True)  11 us
    all_to_all x1, blocking collectives, copy_for_each(): return lax.all_to_all(copies, axis, split_axis=0, concat_axis=0, tiled=True)  7.97 us
    all_to_all x1, blocking collectives, summed_on_arrival(): lax.all_to_all(split_up(shard, dim, devices), axis, 0, 0, tiled=True)  7.57 us
  transfers between devices with their start and end apart: 4, of which 4 were waited for; matrix products, arithmetic and copies ran while one was open for 5% of the time, Pallas kernels for 0%

commit v1 on v0

v1 whole, which is shorter than its diff:
```python
import jax
import jax.numpy as jnp
from jax import lax
from jax.sharding import Mesh
from jax.sharding import PartitionSpec as P

AXES = ("x", "y_hi", "z", "y_lo", "core")
ROW = ("x", "y_hi")
COL = ("z", "y_lo", "core")
FIRST = (((0,), (0,)), ((), ()))
PLAIN = (((1,), (0,)), ((), ()))


def product(first, second, dims=FIRST):
    return lax.dot_general(
        first, second, dims, precision=lax.Precision.HIGH, preferred_element_type=jnp.float32
    )


def swap(block, axis):
    return lax.ppermute(block, axis, [(0, 1), (1, 0)])


def lane_step(block, axis, size):
    pairs = []
    for place in range(size):
        pairs.append((place * 2, (place + 1) % size * 2))
        pairs.append((place * 2 + 1, (place - 1) % size * 2 + 1))
    return lax.ppermute(block, (axis, "core"), pairs)


def local(left_panel, right_panel, arc_basis, normal_block):
    x, y_hi, z, y_lo, core = (lax.axis_index(name) for name in AXES)
    left_rows, right_rows = left_panel.shape[0], right_panel.shape[0]
    half = left_panel.shape[1] // 2
    sizes = {name: lax.axis_size(name) for name in AXES}
    up = 1 - 2 * core
    row_index = x * sizes["y_hi"] + y_hi
    col_index = (z * sizes["y_lo"] + y_lo) * 2 + core

    left_whole = lax.all_gather(left_panel, COL, axis=0, tiled=True)

    mine, other = right_panel, swap(right_panel, "y_hi")
    right_whole = jnp.zeros((arc_basis.shape[0], right_panel.shape[1]), jnp.float32)
    for step in range(sizes["x"]):
        place = lax.rem(x - up * step + sizes["x"], sizes["x"]) * sizes["y_hi"]
        for block, hi in ((mine, y_hi), (other, 1 - y_hi)):
            right_whole = lax.dynamic_update_slice_in_dim(
                right_whole, block, (place + hi) * right_rows, 0
            )
        if step < sizes["x"] - 1:
            mine = lane_step(mine, "x", sizes["x"])
            other = lane_step(other, "x", sizes["x"])

    right_coef = product(arc_basis, right_whole)
    right_kept = right_whole - product(arc_basis, right_coef, PLAIN)
    right_reduced = lax.dynamic_slice_in_dim(right_kept, row_index * right_rows, right_rows, 0)

    own_half = lax.dynamic_slice_in_dim(left_whole, core * half, half, 1)
    coef_half = product(arc_basis, own_half)
    coef_other = swap(coef_half, "core")
    basis_own = lax.dynamic_slice_in_dim(arc_basis, col_index * left_rows, left_rows, 0)
    near = product(basis_own, coef_half, PLAIN)
    far = product(basis_own, coef_other, PLAIN)
    fitted = jnp.where(
        core == 0, jnp.concatenate([near, far], 1), jnp.concatenate([far, near], 1)
    )
    left_reduced = left_panel - fitted
    updated_block = normal_block + product(left_whole, right_kept)
    return (updated_block, left_reduced, right_reduced)


def solution(mesh):
    split = Mesh(mesh.devices.reshape(4, 2, 8, 2, 2), AXES)
    in_specs = (P(COL, ROW), P(ROW, COL), P(), P(ROW, COL))
    out_specs = (P(ROW, COL), P(COL, ROW), P(ROW, COL))
    return jax.shard_map(local, mesh=split, in_specs=in_specs, out_specs=out_specs, check_vma=False)
```

time: 319 us -> 167 us (0.52)
  waiting for transfers between devices: 204 us -> 73.1 us
  blocking collectives: 38.9 us -> 0 us
  local copies, waits for them, and re-layouts: 4.85 us -> 18.7 us
  starting transfers between devices: 11.1 us -> 19.7 us
  matrix products: 43.1 us -> 38.3 us
    all_gather x1, waiting for transfers between devices: 100 us -> 5.76 us  [local(): left_whole = lax.all_gather(left_panel, COL, axis=0, tiled=True)]
    all_to_all x2 -> x0, waiting for transfers between devices: 69.7 us -> none  [copy_for_each(): return lax.all_to_all(copies, axis, split_axis=0, concat_axis=0, tiled=True)]
    ppermute x0 -> x8, waiting for transfers between devices: none -> 66.6 us  [the longest x6 37.9 us: lane_step(): return lax.ppermute(block, (axis, 'core'), pairs)]
    all_to_all x3 -> x0, blocking collectives: 38.9 us -> none  [the longest x1 23.4 us: sum_in_two_steps(): return jnp.sum(lax.all_to_all(own, far, 0, 0, tiled=True), axis=0)]
    all_gather x1 -> x0, waiting for transfers between devices: 32.2 us -> none  [local(): lax.all_gather(right_panel, 'row', axis=0, tiled=True)]
    ppermute x0 -> x8, starting transfers between devices: none -> 19.6 us  [the longest x6 15.5 us: lane_step(): return lax.ppermute(block, (axis, 'core'), pairs)]
    unnamed x6 -> x24, local copies, waits for them, and re-layouts: 0.01 us -> 11.5 us
    all_to_all x2 -> x0, starting transfers between devices: 11 us -> none  [copy_for_each(): return lax.all_to_all(copies, axis, split_axis=0, concat_axis=0, tiled=True)]
  transfers between devices with their start and end apart: 4 -> 9, of which waited for: 4 -> 7; matrix products, arithmetic and copies ran while one was open for 5% -> 25% of each run, Pallas kernels for 0% -> 0%
where the time goes in v1:
time: 167 us; the launch traced here: 165 us
  waiting for transfers between devices  73.1 us (44%)
  matrix products  38.3 us (23%)
  starting transfers between devices  19.7 us (12%)
  local copies, waits for them, and re-layouts  18.7 us (11%)
  between operations  14.3 us (9%)
    dot_general x6, matrix products, product(): lax.dot_general(first, second, dims, precision=lax.Precision.HIGH, prefer...  38.3 us
    ppermute x6, waiting for transfers between devices, lane_step(): return lax.ppermute(block, (axis, 'core'), pairs)  37.9 us
    ppermute x2, waiting for transfers between devices, swap(): return lax.ppermute(block, axis, [(0, 1), (1, 0)])  28.8 us
    ppermute x6, starting transfers between devices, lane_step(): return lax.ppermute(block, (axis, 'core'), pairs)  15.5 us
    unnamed x24, local copies, waits for them, and re-layouts  11.5 us
    dynamic_update_slice x8, local copies, waits for them, and re-layouts, local(): lax.dynamic_update_slice_in_dim(right_whole, block, (place + hi) * right_...  6.1 us
    all_gather x1, waiting for transfers between devices, local(): left_whole = lax.all_gather(left_panel, COL, axis=0, tiled=True)  5.76 us
    ppermute x2, starting transfers between devices, swap(): return lax.ppermute(block, axis, [(0, 1), (1, 0)])  4.19 us
  transfers between devices with their start and end apart: 9, of which 7 were waited for; matrix products, arithmetic and copies ran while one was open for 25% of the time, Pallas kernels for 0%

profile of v1, /device:TPU:1, one launch (start us, length us, event | category | flops | bytes accessed | tf_op | source)
XLA Modules:
  0.0 164.9 jit_solution(7828961570251210467)
XLA Ops:
  7.2 0.0 all-gather.2.cloned.1.call-start
  7.2 0.7 all-gather.2.cloned.1.call-update
  7.9 1.6 copy.7
  9.5 3.8 %collective-permute-start = (f32[512,512]{0,1:T(8,128)S(1)}, f32[512,512]{0,1:T(8,128)S(1)}, u32[]{:S(2)}, u32[]{:S(2)}) collective-permute-start(f32[512,512]{0,1:T(8,128)S(1)} %copy.7), channel_id=1, source_target_pairs={{0,32},{32,0},{1,33},{33,1},{2,34},{34,2},{3,35},{35,3},{4,36},{36... | collective-permute-start | bytes 3145736 | tf_op jit(solution)/shard_map/ppermute | solution.py:21
  13.3 2.5 %collective-permute-start.1 = (f32[512,512]{0,1:T(8,128)S(1)}, f32[512,512]{0,1:T(8,128)S(1)}, u32[]{:S(2)}, u32[]{:S(2)}) collective-permute-start(f32[512,512]{0,1:T(8,128)S(1)} %copy.7), channel_id=1, source_target_pairs={{0,64},{1,193},{64,128},{65,1},{128,192},{129,65},{192,0},{193,129... | collective-permute-start | bytes 3145736 | tf_op jit(solution)/shard_map/ppermute | solution.py:29
  15.8 28.8 %collective-permute-done = f32[512,512]{0,1:T(8,128)S(1)} collective-permute-done((f32[512,512]{0,1:T(8,128)S(1)}, f32[512,512]{0,1:T(8,128)S(1)}, u32[]{:S(2)}, u32[]{:S(2)}) %collective-permute-start) | collective-permute-done | bytes 1048608 | tf_op jit(solution)/shard_map/ppermute | solution.py:21
  44.6 2.5 %collective-permute-start.2 = (f32[512,512]{0,1:T(8,128)S(1)}, f32[512,512]{0,1:T(8,128)S(1)}, u32[]{:S(2)}, u32[]{:S(2)}) collective-permute-start(f32[512,512]{0,1:T(8,128)S(1)} %collective-permute-done), channel_id=1, source_target_pairs={{0,64},{1,193},{64,128},{65,1},{128,192},{129,65},{192,0},{193,129... | collective-permute-start | bytes 3145736 | tf_op jit(solution)/shard_map/ppermute | solution.py:29
  47.0 0.0 collective-permute-done.1
  47.0 1.0 collective-permute-start.3
  48.0 10.8 %collective-permute-done.2 = f32[512,512]{0,1:T(8,128)S(1)} collective-permute-done((f32[512,512]{0,1:T(8,128)S(1)}, f32[512,512]{0,1:T(8,128)S(1)}, u32[]{:S(2)}, u32[]{:S(2)}) %collective-permute-start.2) | collective-permute-done | bytes 1048608 | tf_op jit(solution)/shard_map/ppermute | solution.py:29
  58.8 3.1 %collective-permute-start.4 = (f32[512,512]{0,1:T(8,128)S(1)}, f32[512,512]{0,1:T(8,128)}, u32[]{:S(2)}, u32[]{:S(2)}) collective-permute-start(f32[512,512]{0,1:T(8,128)S(1)} %collective-permute-done.2), channel_id=1, source_target_pairs={{0,64},{1,193},{64,128},{65,1},{128,192},{129,65},{192,0},{193,129... | collective-permute-start | bytes 3145736 | tf_op jit(solution)/shard_map/ppermute | solution.py:29
  61.9 8.1 %collective-permute-done.3 = f32[512,512]{0,1:T(8,128)} collective-permute-done((f32[512,512]{0,1:T(8,128)S(1)}, f32[512,512]{0,1:T(8,128)}, u32[]{:S(2)}, u32[]{:S(2)}) %collective-permute-start.3) | collective-permute-done | bytes 1048608 | tf_op jit(solution)/shard_map/ppermute | solution.py:29
  70.0 3.2 %collective-permute-start.5 = (f32[512,512]{0,1:T(8,128)}, f32[512,512]{0,1:T(8,128)}, u32[]{:S(2)}, u32[]{:S(2)}) collective-permute-start(f32[512,512]{0,1:T(8,128)} %collective-permute-done.3), channel_id=1, source_target_pairs={{0,64},{1,193},{64,128},{65,1},{128,192},{129,65},{192,0},{193,129... | collective-permute-start | bytes 3145736 | tf_op jit(solution)/shard_map/ppermute | solution.py:29
  73.2 8.0 %collective-permute-done.4 = f32[512,512]{0,1:T(8,128)} collective-permute-done((f32[512,512]{0,1:T(8,128)S(1)}, f32[512,512]{0,1:T(8,128)}, u32[]{:S(2)}, u32[]{:S(2)}) %collective-permute-start.4) | collective-permute-done | bytes 1048608 | tf_op jit(solution)/shard_map/ppermute | solution.py:29
  81.2 3.2 %collective-permute-start.6 = (f32[512,512]{0,1:T(8,128)}, f32[512,512]{0,1:T(8,128)}, u32[]{:S(2)}, u32[]{:S(2)}) collective-permute-start(f32[512,512]{0,1:T(8,128)} %collective-permute-done.4), channel_id=1, source_target_pairs={{0,64},{1,193},{64,128},{65,1},{128,192},{129,65},{192,0},{193,129... | collective-permute-start | bytes 3145736 | tf_op jit(solution)/shard_map/ppermute | solution.py:29
  84.5 1.9 %copy.10 = f32[1024,512]{0,1:T(8,128)S(1)} copy(f32[1024,512]{1,0:T(8,128)} %param.7) | data formatting | bytes 4194304 | tf_op args[3]
  86.4 0.0 copy-start.5
  86.5 0.0 copy-start.7
  86.5 1.0 broadcast_in_dim.3
  87.5 0.0 copy-start
  87.5 0.1 constant_dynamic-update-slice_fusion.7
  87.6 0.1 copy-done.5
  87.7 0.1 constant_dynamic-update-slice_fusion.6
  87.8 0.3 copy-done.7
  88.0 0.1 constant_dynamic-update-slice_fusion.5
  88.2 0.2 copy-done.9
  88.4 0.1 constant_dynamic-update-slice_fusion.4
  88.5 1.6 constant_dynamic-update-slice_fusion.3
  90.1 1.3 constant_dynamic-update-slice_fusion.2
  91.5 1.1 collective-permute-done.5
  92.6 1.4 constant_dynamic-update-slice_fusion.1
  94.0 9.8 %collective-permute-done.6 = f32[512,512]{0,1:T(8,128)} collective-permute-done((f32[512,512]{0,1:T(8,128)}, f32[512,512]{0,1:T(8,128)}, u32[]{:S(2)}, u32[]{:S(2)}) %collective-permute-start.6) | collective-permute-done | bytes 1048608 | tf_op jit(solution)/shard_map/ppermute | solution.py:29
  103.8 1.4 constant_dynamic-update-slice_fusion
  105.2 3.7 %fusion.10 = f32[512,256]{1,0:T(8,128)S(1)} fusion(f32[4096,512]{0,1:T(8,128)S(1)} %constant_dynamic-update-slice_fusion, f32[4096,256]{1,0:T(8,128)S(1)} %copy-done), kind=kOutput, calls=%fused_computation.22 | convolution fusion | flops 3221225472 | bytes 13107200 | tf_op jit(solution)/shard_map/dot_general | solution.py:15
  108.9 4.2 %bitcast_subtract_fusion = f32[4096,512]{0,1:T(8,128)S(1)} fusion(f32[4096,512]{0,1:T(8,128)S(1)} %constant_dynamic-update-slice_fusion, f32[512,256]{1,0:T(8,128)S(1)} %fusion.10, f32[4096,256]{1,0:T(8,128)S(1)} %copy-done), kind=kOutput, calls=%fused_computation | convolution fusion | flops 3223322624 | bytes 21495808 | tf_op jit(solution)/shard_map/dot_general | solution.py:15
  113.1 3.2 %copy-done.1 = f32[4096,512]{0,1:T(8,128)} copy-done((f32[4096,512]{0,1:T(8,128)}, f32[4096,512]{0,1:T(8,128)S(1)}, u32[]{:S(2)}) %copy-start.1) | copy-done | bytes 8388632
  116.3 0.1 constant_dynamic-slice_fusion
  116.4 1.3 copy.12
  117.7 5.8 %all-gather.2.cloned.1.call-done = f32[4096,1024]{1,0:T(8,128)} async-done(((f32[128,1024]{1,0:T(8,128)}), f32[4096,1024]{1,0:T(8,128)}) %all-gather.2.cloned.1.call-update) | async-done | bytes 16777232 | tf_op jit(solution)/shard_map/all_gather | solution.py:41
  123.5 10.5 %fusion = f32[512,256]{1,0:T(8,128)S(1)} fusion(f32[4096,256]{1,0:T(8,128)} %param.6, f32[4096,1024]{1,0:T(8,128)} %all-gather.2.cloned.1.call-done, s32[]{:T(128)S(6)} %select_n.51), kind=kOutput, calls=%fused_computation.1 | convolution fusion | flops 3221225472 | bytes 13107204 | tf_op jit(solution)/shard_map/dot_general | solution.py:15
  134.0 0.0 copy-start.3
  134.0 0.4 collective-permute-start.7
  134.4 17.1 %bitcast_add_fusion = f32[1024,512]{0,1:T(8,128)} fusion(f32[1024,512]{0,1:T(8,128)S(1)} %copy.10, f32[4096,512]{0,1:T(8,128)S(1)} %copy-done.2, f32[4096,1024]{1,0:T(8,128)} %all-gather.2.cloned.1.call-done), kind=kOutput, calls=%fused_computation.3 | convolution fusion | flops 12885426176 | bytes 29360128 | tf_op jit(solution)/shard_map/dot_general | solution.py:15
  151.4 2.9 %copy.11 = f32[1024,512]{1,0:T(8,128)} copy(f32[1024,512]{0,1:T(8,128)} %bitcast_add_fusion) | data formatting | bytes 4194304
  154.3 1.3 fusion.5
  155.6 0.0 collective-permute-done.7
  155.6 1.5 fusion.3
  157.2 0.9 fusion.2
  (12 shorter events, 0.0 us)
Async XLA Ops:
  7.2 116.3 %all-gather.2.cloned.1.call-start = ((), (), s32[]{:S(2)}) async-start(), calls=%async_computation | async-start | bytes 17301504 | tf_op jit(solution)/shard_map/all_gather | solution.py:41
  9.5 35.1 %collective-permute-start = (f32[512,512]{0,1:T(8,128)S(1)}, f32[512,512]{0,1:T(8,128)S(1)}, u32[]{:S(2)}, u32[]{:S(2)}) collective-permute-start(f32[512,512]{0,1:T(8,128)S(1)} %copy.7), channel_id=1, source_target_pairs={{0,32},{32,0},{1,33},{33,1},{2,34},{34,2},{3,35},{35,3},{4,36},{36... | collective-permute-start | bytes 3145736 | tf_op jit(solution)/shard_map/ppermute | solution.py:21
  13.3 33.7 %collective-permute-start.1 = (f32[512,512]{0,1:T(8,128)S(1)}, f32[512,512]{0,1:T(8,128)S(1)}, u32[]{:S(2)}, u32[]{:S(2)}) collective-permute-start(f32[512,512]{0,1:T(8,128)S(1)} %copy.7), channel_id=1, source_target_pairs={{0,64},{1,193},{64,128},{65,1},{128,192},{129,65},{192,0},{193,129... | collective-permute-start | bytes 3145736 | tf_op jit(solution)/shard_map/ppermute | solution.py:29
  44.5 2.5 %copy-start.4 = (f32[512,512]{0,1:T(8,128)}, f32[512,512]{0,1:T(8,128)S(1)}, u32[]{:S(2)}) copy-start(f32[512,512]{0,1:T(8,128)S(1)} %collective-permute-done) | copy-start | bytes 3145732
  44.6 14.2 %collective-permute-start.2 = (f32[512,512]{0,1:T(8,128)S(1)}, f32[512,512]{0,1:T(8,128)S(1)}, u32[]{:S(2)}, u32[]{:S(2)}) collective-permute-start(f32[512,512]{0,1:T(8,128)S(1)} %collective-permute-done), channel_id=1, source_target_pairs={{0,64},{1,193},{64,128},{65,1},{128,192},{129,65},{192,0},{193,129... | collective-permute-start | bytes 3145736 | tf_op jit(solution)/shard_map/ppermute | solution.py:29
  47.0 11.7 %copy-start.6 = (f32[512,512]{0,1:T(8,128)}, f32[512,512]{0,1:T(8,128)S(1)}, u32[]{:S(2)}) copy-start(f32[512,512]{0,1:T(8,128)S(1)} %collective-permute-done.1) | copy-start | bytes 3145732
  47.0 23.0 %collective-permute-start.3 = (f32[512,512]{0,1:T(8,128)S(1)}, f32[512,512]{0,1:T(8,128)}, u32[]{:S(2)}, u32[]{:S(2)}) collective-permute-start(f32[512,512]{0,1:T(8,128)S(1)} %collective-permute-done.1), channel_id=1, source_target_pairs={{0,64},{1,193},{64,128},{65,1},{128,192},{129,65},{192,0},{193,129... | collective-permute-start | bytes 3145736 | tf_op jit(solution)/shard_map/ppermute | solution.py:29
  58.8 11.2 %copy-start.8 = (f32[512,512]{0,1:T(8,128)}, f32[512,512]{0,1:T(8,128)S(1)}, u32[]{:S(2)}) copy-start(f32[512,512]{0,1:T(8,128)S(1)} %collective-permute-done.2) | copy-start | bytes 3145732
  58.8 22.5 %collective-permute-start.4 = (f32[512,512]{0,1:T(8,128)S(1)}, f32[512,512]{0,1:T(8,128)}, u32[]{:S(2)}, u32[]{:S(2)}) collective-permute-start(f32[512,512]{0,1:T(8,128)S(1)} %collective-permute-done.2), channel_id=1, source_target_pairs={{0,64},{1,193},{64,128},{65,1},{128,192},{129,65},{192,0},{193,129... | collective-permute-start | bytes 3145736 | tf_op jit(solution)/shard_map/ppermute | solution.py:29
  70.0 22.6 %collective-permute-start.5 = (f32[512,512]{0,1:T(8,128)}, f32[512,512]{0,1:T(8,128)}, u32[]{:S(2)}, u32[]{:S(2)}) collective-permute-start(f32[512,512]{0,1:T(8,128)} %collective-permute-done.3), channel_id=1, source_target_pairs={{0,64},{1,193},{64,128},{65,1},{128,192},{129,65},{192,0},{193,129... | collective-permute-start | bytes 3145736 | tf_op jit(solution)/shard_map/ppermute | solution.py:29
  81.2 22.6 %collective-permute-start.6 = (f32[512,512]{0,1:T(8,128)}, f32[512,512]{0,1:T(8,128)}, u32[]{:S(2)}, u32[]{:S(2)}) collective-permute-start(f32[512,512]{0,1:T(8,128)} %collective-permute-done.4), channel_id=1, source_target_pairs={{0,64},{1,193},{64,128},{65,1},{128,192},{129,65},{192,0},{193,129... | collective-permute-start | bytes 3145736 | tf_op jit(solution)/shard_map/ppermute | solution.py:29
  86.4 1.2 copy-start.5
  86.5 1.6 copy-start.7
  86.5 1.9 %copy-start.9 = (f32[512,512]{0,1:T(8,128)S(1)}, f32[512,512]{0,1:T(8,128)}, u32[]{:S(2)}) copy-start(f32[512,512]{0,1:T(8,128)} %copy-done.8) | copy-start | bytes 3145732
  87.5 17.7 %copy-start = (f32[4096,256]{1,0:T(8,128)S(1)}, f32[4096,256]{1,0:T(8,128)}, u32[]{:S(2)}) copy-start(f32[4096,256]{1,0:T(8,128)} %param.6) | copy-start | bytes 12582916
  113.1 3.2 %copy-start.1 = (f32[4096,512]{0,1:T(8,128)}, f32[4096,512]{0,1:T(8,128)S(1)}, u32[]{:S(2)}) copy-start(f32[4096,512]{0,1:T(8,128)S(1)} %bitcast_subtract_fusion) | copy-start | bytes 25165828
  123.5 10.9 %copy-start.2 = (f32[4096,512]{0,1:T(8,128)S(1)}, f32[4096,512]{0,1:T(8,128)}, u32[]{:S(2)}) copy-start(f32[4096,512]{0,1:T(8,128)} %copy-done.1) | copy-start | bytes 25165828
  134.0 23.2 %copy-start.3 = (f32[128,1024]{1,0:T(8,128)S(1)}, f32[128,1024]{1,0:T(8,128)}, u32[]{:S(2)}) copy-start(f32[128,1024]{1,0:T(8,128)} %param.4) | copy-start | bytes 1572868
  134.0 21.6 %collective-permute-start.7 = (f32[256,512]{0,1:T(8,128)S(1)}, f32[256,512]{0,1:T(8,128)}, u32[]{:S(2)}, u32[]{:S(2)}) collective-permute-start(f32[256,512]{0,1:T(8,128)S(1)} %bitcast.14), channel_id=1, source_target_pairs={{0,1},{1,0},{2,3},{3,2},{4,5},{5,4},{6,7},{7,6},{8,9},{9,8},{10,11... | collective-permute-start | bytes 1572872 | tf_op jit(solution)/shard_map/ppermute | solution.py:21
Sparse Core Ops, SparseCore 0:
  9.9 113.6 all-gather.1
